TPU v7x, 32 devices: a whole 2x2x4 slice. The times are simulated.
32 devices in a mesh: ctx: 8 (over z, y), tp: 4 (over x, core).
Axes of the slice: x: 2, y: 2, z: 4, core: 2. Of those that a mesh axis runs over, the one named last changes fastest.
Arguments:
- tokens: bfloat16 [4096, 5376], P(('ctx', 'tp')), may hold values from -8 to 8
- positions: int32 [4096], replicated, may hold values from 0 to 16383, as said below
- w_query: bfloat16 [5376, 2048], P('ctx', 'tp'), may hold values from -1 to 1
- key_matrix: bfloat16 [5376, 1024], P('ctx', 'tp'), may hold values from -1 to 1
- value_matrix: bfloat16 [5376, 1024], P('ctx', 'tp'), may hold values from -0.078125 to 0.078125
- w_out: bfloat16 [2048, 5376], P('tp', 'ctx'), may hold values from -0.125 to 0.125
- gain_in: float32 [5376], replicated, may hold values from 0.1 to 1.9
- gain_query: float32 [128], replicated, may hold values from 0.5 to 14
- gain_key: float32 [128], replicated, may hold values from 0.5 to 14
- gain_post: float32 [5376], replicated, may hold values from 0.1 to 1.9
Outputs:
- layer_out: bfloat16 [4096, 5376], P(('ctx', 'tp'))
Inputs may be any that keep to these rules, and one draw needn't show every extreme that they name: (positions) rise strictly along the tokens, by 1 to 4 from one token to the next, and the last token stands at 16383.
All inputs are finite; a program needn't handle non-finite values.
Results may differ from a plain program's by a relative error of at most 0.013.
The roundings to bfloat16 on the way count: a program that leaves them out, or rounds other values in their place, can miss the bound.
Values may be sent and summed in bfloat16 or wider, within the bound.
A program may use at most 128 MiB of HBM per device.

v0:
```python
import jax
import jax.numpy as jnp
from jax import lax
from jax.sharding import PartitionSpec as P

HEAD_SIZE = 128
QS = 168
LOOKBACK_WINDOW = 1024


EPSILON = 1e-06
ROPE_BASE = 10000.0


def shifted(value, axis, steps):
    count = lax.axis_size(axis)
    leading, last = (max(0, -steps), min(count, count - steps))
    return lax.ppermute(value, axis, [(source, source + steps) for source in range(leading, last)])


def row_norm(values, scales):
    mean_square = jnp.mean(values * values, axis=-1, keepdims=True)
    return values * lax.rsqrt(mean_square + EPSILON) * scales


def rotate(head_rows, offsets):
    half_dim = head_rows.shape[-1] // 2
    frequency = ROPE_BASE ** (
        -(jnp.arange(half_dim, dtype=jnp.float32) * 2.0) / head_rows.shape[-1]
    )
    angles = offsets.astype(jnp.float32)[:, None] * frequency[None, :]
    cosine = jnp.cos(angles)[:, None, :]
    sine_wave = jnp.sin(angles)[:, None, :]
    first_half = head_rows[..., :half_dim]
    second_half = head_rows[..., half_dim:]
    return jnp.concatenate(
        [
            first_half * cosine - second_half * sine_wave,
            second_half * cosine + first_half * sine_wave,
        ],
        axis=-1,
    )


def attend(query_matrix, projected_keys, projected_values, query_offsets, key_offsets, key_valid):
    scores = jnp.einsum(
        "qkgd,skd->kgqs", query_matrix, projected_keys, preferred_element_type=jnp.float32
    ) * QS ** (-0.5)
    position_gap = query_offsets[:, None] - key_offsets[None, :]
    allowed = key_valid[None, :] & (position_gap >= 0) & (position_gap < LOOKBACK_WINDOW)
    scores = jnp.where(allowed[None, None], scores, -1e30)
    row_max = jnp.max(scores, axis=-1, keepdims=True)
    weights = jnp.where(allowed[None, None], jnp.exp(scores - row_max), 0.0)
    totals = jnp.sum(weights, axis=-1, keepdims=True)
    rounded = weights.astype(jnp.bfloat16)
    mixed = jnp.einsum(
        "kgqs,skd->qkgd", rounded, projected_values, preferred_element_type=jnp.float32
    )
    mixed = mixed / jnp.transpose(totals, (2, 0, 1, 3))
    return mixed.astype(jnp.bfloat16).reshape(query_matrix.shape[0], -1)


def shards(
    tokens,
    positions,
    w_query,
    key_matrix,
    value_matrix,
    w_out,
    gain_in,
    gain_query,
    gain_key,
    gain_post,
):
    gathered = lax.all_gather(tokens, "tp", axis=0, tiled=True)
    normalized_rows = row_norm(gathered.astype(jnp.float32), gain_in).astype(jnp.bfloat16)
    row_count = normalized_rows.shape[0]
    block_start = lax.axis_index("ctx") * row_count
    offsets_all = positions - positions[0]
    query_offsets = lax.dynamic_slice_in_dim(offsets_all, block_start, row_count, 0)

    def add_rows(weight_rows):
        return jnp.dot(normalized_rows, weight_rows, preferred_element_type=jnp.float32)

    query_raw = add_rows(lax.all_gather(w_query, "ctx", axis=0, tiled=True))
    unnormed_keys = add_rows(lax.all_gather(key_matrix, "ctx", axis=0, tiled=True))
    value_raw = add_rows(lax.all_gather(value_matrix, "ctx", axis=0, tiled=True))
    key_heads = key_matrix.shape[1] // HEAD_SIZE
    projected_keys = rotate(
        row_norm(unnormed_keys.reshape(row_count, key_heads, HEAD_SIZE), gain_key), query_offsets
    ).astype(jnp.bfloat16)
    projected_values = value_raw.astype(jnp.bfloat16).reshape(row_count, key_heads, HEAD_SIZE)
    own_pair = jnp.stack([projected_keys, projected_values])
    window_blocks = LOOKBACK_WINDOW // row_count
    earlier = []
    carried = own_pair
    for relay_step in range(window_blocks):
        carried = shifted(carried, "ctx", 1)
        earlier.insert(0, carried)
    window_pair = jnp.concatenate(earlier + [own_pair], axis=1)
    query_heads = w_query.shape[1] // HEAD_SIZE
    query_matrix = rotate(
        row_norm(query_raw.reshape(row_count, query_heads, HEAD_SIZE), gain_query), query_offsets
    ).astype(jnp.bfloat16)
    query_matrix = query_matrix.reshape(row_count, key_heads, query_heads // key_heads, HEAD_SIZE)
    padded_offsets = jnp.concatenate(
        [jnp.zeros((LOOKBACK_WINDOW,), jnp.int32), offsets_all], axis=0
    )
    key_offsets = lax.dynamic_slice_in_dim(
        padded_offsets, block_start, LOOKBACK_WINDOW + row_count, 0
    )
    key_valid = (
        block_start + jnp.arange(LOOKBACK_WINDOW + row_count, dtype=jnp.int32) >= LOOKBACK_WINDOW
    )
    attended = attend(
        query_matrix, window_pair[0], window_pair[1], query_offsets, key_offsets, key_valid
    )
    projected = jnp.dot(
        attended,
        lax.all_gather(w_out, "ctx", axis=1, tiled=True),
        preferred_element_type=jnp.float32,
    )
    summed = lax.psum_scatter(
        projected.astype(jnp.bfloat16), "tp", scatter_dimension=0, tiled=True
    ).astype(jnp.float32)
    return (tokens.astype(jnp.float32) + row_norm(summed, gain_post)).astype(jnp.bfloat16)


def solution(mesh):
    in_specs = (
        P(("ctx", "tp"), None),
        P(),
        P("ctx", "tp"),
        P("ctx", "tp"),
        P("ctx", "tp"),
        P("tp", "ctx"),
        P(),
        P(),
        P(),
        P(),
    )
    out_specs = P(("ctx", "tp"), None)
    return jax.shard_map(shards, mesh=mesh, in_specs=in_specs, out_specs=out_specs, check_vma=False)
```

profile of v0, /device:TPU:0, one launch (start us, length us, event | category | flops | bytes accessed | tf_op | source)
XLA Modules:
  0.0 434.3 jit_solution(12205699914672215212)
XLA Ops:
  10.0 1.2 slice.22
  11.2 1.4 broadcast_subtract_fusion
  13.4 40.1 %all-gather.6.cloned.1.call-done = bf16[512,5376]{1,0:T(8,128)(2,1)} async-done(((bf16[128,5376]{1,0:T(8,128)(2,1)}), bf16[512,5376]{1,0:T(8,128)(2,1)}) %all-gather.6.cloned.1.call-update) | async-done | bytes 5505040 | tf_op jit(solution)/shard_map/all_gather | solution.py:75
  53.5 3.7 fusion.1
  57.3 54.5 %all-gather.8.cloned.1.call-done = bf16[5376,256]{1,0:T(8,128)(2,1)} async-done(((bf16[672,256]{1,0:T(8,128)(2,1)}), bf16[5376,256]{1,0:T(8,128)(2,1)}) %all-gather.8.cloned.1.call-update) | async-done | bytes 2752528 | tf_op jit(solution)/shard_map/all_gather | solution.py:86
  111.8 5.4 %multiply_reduce_fusion.1 = (f32[512,2]{0,1:T(2,128)S(1)}, f32[512,256]{0,1:T(8,128)S(1)}) fusion(bf16[5376,256]{1,0:T(8,128)(2,1)} %all-gather.8.cloned.1.call-done, bf16[512,5376]{1,0:T(8,128)(2,1)} %all-gather.6.cloned.1.call-done, f32[5376]{0:T(1024)S(1)} %copy-done.5, f32[512]{0:T(512)S(1)} %add_rsqrt_fusion.2), kind=kOutput, calls=%fused_computation.43 | convolution fusion | flops 1420557312 | bytes 8809472 | tf_op jit(solution)/shard_map/dot_general | solution.py:83
  117.4 51.2 %all-gather.10.cloned.1.call-done = bf16[5376,256]{1,0:T(8,128)(2,1)} async-done(((bf16[672,256]{1,0:T(8,128)(2,1)}), bf16[5376,256]{1,0:T(8,128)(2,1)}) %all-gather.10.cloned.1.call-update) | async-done | bytes 2752528 | tf_op jit(solution)/shard_map/all_gather | solution.py:87
  168.6 5.4 %convolution_convert_fusion.1 = bf16[512,256]{0,1:T(8,128)(2,1)S(1)} fusion(bf16[5376,256]{1,0:T(8,128)(2,1)} %all-gather.10.cloned.1.call-done, bf16[512,5376]{1,0:T(8,128)(2,1)} %all-gather.6.cloned.1.call-done, f32[5376]{0:T(1024)S(1)} %copy-done.5, f32[512]{0:T(512)S(1)} %add_rsqrt_fusion.2), kind=kOutput, calls=%fused_computation.30 | convolution fusion | flops 1420427264 | bytes 8543232 | tf_op jit(solution)/shard_map/dot_general | solution.py:83
  174.8 2.5 collective-permute-start
  177.4 16.8 %collective-permute-done = bf16[2,512,2,128]{3,1,2,0:T(8,128)(2,1)S(1)} collective-permute-done((bf16[2,512,2,128]{3,1,2,0:T(8,128)(2,1)S(1)}, bf16[2,512,2,128]{3,1,2,0:T(8,128)(2,1)S(1)}, u32[]{:S(2)}, u32[]{:S(2)}) %collective-permute-start) | collective-permute-done | bytes 524320 | tf_op jit(solution)/shard_map/ppermute | solution.py:18
  194.2 9.1 %collective-permute-start.1 = (bf16[2,512,2,128]{3,1,2,0:T(8,128)(2,1)S(1)}, bf16[2,512,2,128]{3,1,2,0:T(8,128)(2,1)S(1)}, u32[]{:S(2)}, u32[]{:S(2)}) collective-permute-start(bf16[2,512,2,128]{3,1,2,0:T(8,128)(2,1)S(1)} %collective-permute-done), channel_id=1, source_target_pairs={{0,4},{4,8},{8,12},{12,16},{16,20},{20,24},{24,28},{1,5},{5,9},{9,... | collective-permute-start | bytes 1572872 | tf_op jit(solution)/shard_map/ppermute | solution.py:18
  203.3 1.3 fusion.11
  204.5 5.2 %collective-permute-done.1 = bf16[2,512,2,128]{3,1,2,0:T(8,128)(2,1)S(1)} collective-permute-done((bf16[2,512,2,128]{3,1,2,0:T(8,128)(2,1)S(1)}, bf16[2,512,2,128]{3,1,2,0:T(8,128)(2,1)S(1)}, u32[]{:S(2)}, u32[]{:S(2)}) %collective-permute-start.1) | collective-permute-done | bytes 524320 | tf_op jit(solution)/shard_map/ppermute | solution.py:18
  209.7 1.2 maximum_maximum_fusion
  211.0 63.6 %all-gather.12.cloned.1.call-done = bf16[5376,512]{1,0:T(8,128)(2,1)} async-done(((bf16[672,512]{1,0:T(8,128)(2,1)}), bf16[5376,512]{1,0:T(8,128)(2,1)}) %all-gather.12.cloned.1.call-update) | async-done | bytes 5505040 | tf_op jit(solution)/shard_map/all_gather | solution.py:85
  274.5 8.0 %multiply_reduce_fusion = (f32[512,4]{0,1:T(4,128)S(1)}, f32[512,512]{0,1:T(8,128)S(1)}) fusion(bf16[5376,512]{1,0:T(8,128)(2,1)} %all-gather.12.cloned.1.call-done, bf16[512,5376]{1,0:T(8,128)(2,1)} %all-gather.6.cloned.1.call-done, f32[5376]{0:T(1024)S(1)} %copy-done.5, f32[512]{0:T(512)S(1)} %add_rsqrt_fusion.2), kind=kOutput, calls=%fused_computation.32 | convolution fusion | flops 2830104576 | bytes 12090368 | tf_op jit(solution)/shard_map/dot_general | solution.py:83
  283.0 1.0 copy.23
  284.2 9.1 %fusion.42 = (f32[2,2,512]{2,1,0:T(2,128)S(1)}, bf16[2,2,512,1536]{2,3,1,0:T(8,128)(2,1)}) fusion(pred[512,1536]{0,1:T(8,128)(4,1)S(1)} %fusion.11, bf16[2,1536,2,128]{3,1,2,0:T(8,128)(2,1)S(1)} %maximum_maximum_fusion, bf16[512,2,2,64]{3,0,2,1:T(8,128)(2,1)S(1)} %bitcast.65, bf16[512,2,2,64]{3,0,2,1:T(8,128)(2,1)} %bitcast.64), kind=kOutput, calls=%fused_computation.63 | convolution fusion | flops 825230848 | bytes 9183232 | tf_op jit(solution)/shard_map/sub | solution.py:53
  293.3 3.9 fusion.24
  297.2 66.7 %all-gather.14.cloned.1.call-done = bf16[512,5376]{0,1:T(8,128)(2,1)} async-done(((bf16[512,672]{0,1:T(8,128)(2,1)}), bf16[512,5376]{0,1:T(8,128)(2,1)}) %all-gather.14.cloned.1.call-update) | async-done | bytes 5505040 | tf_op jit(solution)/shard_map/all_gather | solution.py:120
  363.9 7.5 %convolution_convert_fusion = bf16[512,5376]{1,0:T(8,128)(2,1)} fusion(bf16[512,512]{0,1:T(8,128)(2,1)S(1)} %bitcast.68, bf16[512,5376]{0,1:T(8,128)(2,1)} %all-gather.14.cloned.1.call-done), kind=kOutput, calls=%fused_computation.9 | convolution fusion | flops 2821324800 | bytes 11534336 | tf_op jit(solution)/shard_map/dot_general | solution.py:118
  371.4 51.3 %reduce-scatter.2.cloned.1.call-done = bf16[128,5376]{1,0:T(8,128)(2,1)} async-done(((bf16[512,5376]{1,0:T(8,128)(2,1)}), bf16[128,5376]{1,0:T(8,128)(2,1)}) %reduce-scatter.2.cloned.1.call-update) | async-done | bytes 1376272 | tf_op jit(solution)/shard_map/reduce_scatter | solution.py:123
  422.7 1.7 fusion.12
  424.4 3.0 fusion.15
  (43 shorter events, 6.0 us)
Async XLA Ops:
  6.5 105.2 %copy-start.5 = (f32[5376]{0:T(1024)S(1)}, f32[5376]{0:T(1024)}, u32[]{:S(2)}) copy-start(f32[5376]{0:T(1024)} %param.16) | copy-start | bytes 64516
  6.5 47.0 %all-gather.6.cloned.1.call-start = ((), (), s32[]{:S(2)}) async-start(), calls=%async_computation.1 | async-start | bytes 6881280 | tf_op jit(solution)/shard_map/all_gather | solution.py:75
  7.3 104.5 %all-gather.8.cloned.1.call-start = ((), (), s32[]{:S(2)}) async-start(), calls=%async_computation.2 | async-start | bytes 3096576 | tf_op jit(solution)/shard_map/all_gather | solution.py:86
  8.0 160.6 %all-gather.10.cloned.1.call-start = ((), (), s32[]{:S(2)}) async-start(), calls=%async_computation.3 | async-start | bytes 3096576 | tf_op jit(solution)/shard_map/all_gather | solution.py:87
  8.7 265.8 %all-gather.12.cloned.1.call-start = ((), (), s32[]{:S(2)}) async-start(), calls=%async_computation.4 | async-start | bytes 6193152 | tf_op jit(solution)/shard_map/all_gather | solution.py:85
  9.3 354.5 %all-gather.14.cloned.1.call-start = ((), (), s32[]{:S(2)}) async-start(), calls=%async_computation.5 | async-start | bytes 6193152 | tf_op jit(solution)/shard_map/all_gather | solution.py:120
  9.9 412.8 %reduce-scatter.2.cloned.1.call-start = ((), (), s32[]{:S(2)}) async-start(), calls=%async_computation.6 | async-start | bytes 6881280 | tf_op jit(solution)/shard_map/reduce_scatter | solution.py:123
  117.4 56.8 %copy-start.3 = (f32[128]{0:T(128)S(1)}, f32[128]{0:T(128)}, u32[]{:S(2)}) copy-start(f32[128]{0:T(128)} %param.18) | copy-start | bytes 1540
  174.8 19.4 %collective-permute-start = (bf16[2,512,2,128]{3,1,2,0:T(8,128)(2,1)S(1)}, bf16[2,512,2,128]{3,1,2,0:T(8,128)(2,1)S(1)}, u32[]{:S(2)}, u32[]{:S(2)}) collective-permute-start(bf16[2,512,2,128]{3,1,2,0:T(8,128)(2,1)S(1)} %pad_maximum_fusion), channel_id=1, source_target_pairs={{0,4},{4,8},{8,12},{12,16},{16,20},{20,24},{24,28},{1,5},{5,9},{9,... | collective-permute-start | bytes 1572872 | tf_op jit(solution)/shard_map/ppermute | solution.py:18
  194.2 10.4 %copy-start.1 = (bf16[2,512,2,128]{3,1,2,0:T(8,128)(2,1)}, bf16[2,512,2,128]{3,1,2,0:T(8,128)(2,1)S(1)}, u32[]{:S(2)}) copy-start(bf16[2,512,2,128]{3,1,2,0:T(8,128)(2,1)S(1)} %collective-permute-done) | copy-start | bytes 1572868
  194.2 15.5 %collective-permute-start.1 = (bf16[2,512,2,128]{3,1,2,0:T(8,128)(2,1)S(1)}, bf16[2,512,2,128]{3,1,2,0:T(8,128)(2,1)S(1)}, u32[]{:S(2)}, u32[]{:S(2)}) collective-permute-start(bf16[2,512,2,128]{3,1,2,0:T(8,128)(2,1)S(1)} %collective-permute-done), channel_id=1, source_target_pairs={{0,4},{4,8},{8,12},{12,16},{16,20},{20,24},{24,28},{1,5},{5,9},{9,... | collective-permute-start | bytes 1572872 | tf_op jit(solution)/shard_map/ppermute | solution.py:18
  211.0 71.6 %copy-start.4 = (f32[128]{0:T(128)S(1)}, f32[128]{0:T(128)}, u32[]{:S(2)}) copy-start(f32[128]{0:T(128)} %param.17) | copy-start | bytes 1540
  371.4 53.0 %copy-start = (bf16[128,5376]{1,0:T(8,128)(2,1)S(1)}, bf16[128,5376]{1,0:T(8,128)(2,1)}, u32[]{:S(2)}) copy-start(bf16[128,5376]{1,0:T(8,128)(2,1)} %param.10) | copy-start | bytes 4128772
  371.4 53.1 %copy-start.2 = (f32[5376]{0:T(1024)S(1)}, f32[5376]{0:T(1024)}, u32[]{:S(2)}) copy-start(f32[5376]{0:T(1024)} %param.19) | copy-start | bytes 64516
Sparse Core Ops, SparseCore 0:
  8.9 44.6 all-gather.5
  55.7 55.9 all-gather.7
  114.0 54.5 all-gather.9
  170.6 103.8 all-gather.11
  276.6 87.2 all-gather.13
  371.5 51.1 reduce-scatter.1
where the time goes:
time: 435 us; the launch traced here: 434 us
  waiting for transfers between devices  353 us (81%)
  matrix products  39.2 us (9%)
  other arithmetic  13.9 us (3%)
  between operations  13.7 us (3%)
  starting transfers between devices  11.8 us (3%)
    all_gather x1, waiting for transfers between devices, shards(): lax.all_gather(w_out, 'ctx', axis=1, tiled=True)  66.7 us
    all_gather x1, waiting for transfers between devices, shards(): query_raw = add_rows(lax.all_gather(w_query, 'ctx', axis=0, tiled=True))  63.6 us
    all_gather x1, waiting for transfers between devices, shards(): lax.all_gather(key_matrix, 'ctx', axis=0, tiled=True)  54.5 us
    reduce_scatter x1, waiting for transfers between devices, shards(): lax.psum_scatter(projected.astype(jnp.bfloat16), 'tp', scatter_dimension=...  51.3 us
    all_gather x1, waiting for transfers between devices, shards(): lax.all_gather(value_matrix, 'ctx', axis=0, tiled=True)  51.2 us
    all_gather x1, waiting for transfers between devices, shards(): gathered = lax.all_gather(tokens, 'tp', axis=0, tiled=True)  40.1 us
    ppermute x2, waiting for transfers between devices, shifted(): lax.ppermute(value, axis, [(source, source + steps) for source in range(l...  22 us
    dot_general x3, matrix products, add_rows(): jnp.dot(normalized_rows, weight_rows, preferred_element_type=jnp.float32)  18.8 us
  transfers between devices with their start and end apart: 8, of which 8 were waited for; matrix products, arithmetic and copies ran while one was open for 10% of the time, Pallas kernels for 0%

commit v1 on v0

--- a/solution.py
+++ b/solution.py
@@ -1,6 +1,8 @@
 import jax
 import jax.numpy as jnp
 from jax import lax
+from jax.experimental import pallas as pl
+from jax.experimental.pallas import tpu as pltpu
 from jax.sharding import PartitionSpec as P
 
 HEAD_SIZE = 128
@@ -40,6 +42,212 @@
         ],
         axis=-1,
     )
+
+
+PIECES = 6
+Z_SIZE = 4
+MESH = pl.DeviceIdType.MESH
+
+
+def gather_kernel(
+    x_ref, q_ref, k_ref, v_ref, xg_ref, wg_ref,
+    xs, ws, stage_sem, x_send, x_recv, y_send, y_recv, up_send, down_send, below_recv, above_recv,
+):
+    ctx = lax.axis_index("ctx")
+    tp = lax.axis_index("tp")
+    z, y = ctx // 2, ctx % 2
+    y_other = 1 - y
+    core_peer = tp + 1 - 2 * (tp % 2)
+    x_peer = (tp + 2) % 4
+    depth = q_ref.shape[0]
+    piece = depth // PIECES
+    tokens_own = x_ref.shape[0]
+    q_width, k_width = q_ref.shape[1], k_ref.shape[1]
+    y_id = (z * 2 + y_other, tp)
+    up_id = (ctx + 2, tp)
+    down_id = (ctx - 2, tp)
+    core_id = (ctx, core_peer)
+    x_id = (ctx, x_peer)
+
+    barrier = pltpu.get_barrier_semaphore()
+
+    def greet(target):
+        pl.semaphore_signal(barrier, inc=1, device_id=target, device_id_type=MESH)
+
+    greet(y_id)
+    greet(core_id)
+    greet(x_id)
+
+    @pl.when(z < Z_SIZE - 1)
+    def _():
+        greet(up_id)
+
+    @pl.when(z > 0)
+    def _():
+        greet(down_id)
+
+    loads = [
+        pltpu.make_async_copy(q_ref, ws.at[:, pl.ds(0, q_width)], stage_sem.at[0]),
+        pltpu.make_async_copy(k_ref, ws.at[:, pl.ds(q_width, k_width)], stage_sem.at[1]),
+        pltpu.make_async_copy(v_ref, ws.at[:, pl.ds(q_width + k_width, k_width)], stage_sem.at[2]),
+        pltpu.make_async_copy(x_ref, xs, stage_sem.at[3]),
+    ]
+    for copy in loads:
+        copy.start()
+    for copy in loads:
+        copy.wait()
+
+    pl.semaphore_wait(barrier, 4 + ((z + 1) // 2) % 2)
+
+    def rows(owner, part):
+        return wg_ref.at[pl.ds(pl.multiple_of(owner * depth + part * piece, 16), piece)]
+
+    def own_part(part):
+        return ws.at[pl.ds(part * piece, piece)]
+
+    def remote(source, target, send, recv, device):
+        return pltpu.make_async_remote_copy(
+            src_ref=source, dst_ref=target, send_sem=send, recv_sem=recv,
+            device_id=device, device_id_type=MESH,
+        )
+
+    def place(plane, part):
+        if part < PIECES:
+            return rows(plane * 2 + y, part)
+        return rows(plane * 2 + y_other, PIECES - 1)
+
+    def y_copy(plane, part, own=False):
+        target = rows(plane * 2 + y, part)
+        if part == PIECES - 1:
+            slot = Z_SIZE * (PIECES - 1)
+        else:
+            slot = plane * (PIECES - 1) + part
+        return remote(
+            own_part(part) if own else target, target, y_send.at[slot], y_recv.at[slot], y_id
+        )
+
+    def z_copy(plane, distance, part, upward):
+        target = place(plane, part)
+        source = own_part(part) if distance == 0 and part < PIECES else target
+        slot = distance * (PIECES + 1) + part
+        if upward:
+            return remote(source, target, up_send.at[slot], below_recv.at[slot], up_id)
+        return remote(source, target, down_send.at[slot], above_recv.at[slot], down_id)
+
+    def arrived(plane, distance, part, from_below):
+        target = place(plane, part)
+        slot = (distance - 1) * (PIECES + 1) + part
+        if from_below:
+            return remote(target, target, up_send.at[slot], below_recv.at[slot], down_id)
+        return remote(target, target, down_send.at[slot], above_recv.at[slot], up_id)
+
+    def token_rows(owner):
+        return xg_ref.at[pl.ds(pl.multiple_of(owner * tokens_own, 16), tokens_own)]
+
+    def x_copy(owner, slot, device, own):
+        target = token_rows(owner)
+        return remote(xs if own else target, target, x_send.at[slot], x_recv.at[slot], device)
+
+    def send_z(distance, part):
+        @pl.when(z < Z_SIZE - 1)
+        def _():
+            z_copy(z, distance, part, True).start()
+
+        @pl.when(z > 0)
+        def _():
+            z_copy(z, distance, part, False).start()
+
+    y_copy(z, PIECES - 1, own=True).start()
+    x_copy(tp, 0, x_id, True).start()
+    x_copy(tp, 1, core_id, True).start()
+    for part in range(PIECES - 1):
+        send_z(0, part)
+        y_copy(z, part, own=True).start()
+    send_z(0, PIECES - 1)
+    keep = [
+        pltpu.make_async_copy(
+            ws, wg_ref.at[pl.ds(pl.multiple_of(ctx * depth, 16), depth)], stage_sem.at[0]
+        ),
+        pltpu.make_async_copy(xs, token_rows(tp), stage_sem.at[3]),
+    ]
+    for copy in keep:
+        copy.start()
+    y_copy(z, PIECES - 1).wait_recv()
+    send_z(0, PIECES)
+
+    for distance in range(1, Z_SIZE):
+        for part in range(PIECES + 1):
+            @pl.when(z >= distance)
+            def _():
+                arrived(z - distance, distance, part, True).wait_recv()
+                if distance < Z_SIZE - 1:
+                    @pl.when(z < Z_SIZE - 1)
+                    def _():
+                        z_copy(z - distance, distance, part, True).start()
+                if part < PIECES - 1:
+                    y_copy(z - distance, part).start()
+
+            @pl.when(z + distance < Z_SIZE)
+            def _():
+                arrived(z + distance, distance, part, False).wait_recv()
+                if distance < Z_SIZE - 1:
+                    @pl.when(z > 0)
+                    def _():
+                        z_copy(z + distance, distance, part, False).start()
+                if part < PIECES - 1:
+                    y_copy(z + distance, part).start()
+        if distance == 1:
+            x_copy(x_peer, 0, x_id, False).wait_recv()
+            x_copy(x_peer, 2, core_id, False).start()
+
+    x_copy(tp, 1, core_id, False).wait_recv()
+    x_copy(x_peer, 2, core_id, False).wait_recv()
+    for plane in range(Z_SIZE):
+        for part in range(PIECES - 1):
+            y_copy(plane, part).wait_recv()
+    for plane in range(Z_SIZE):
+        for part in range(PIECES - 1):
+            y_copy(plane, part).wait_send()
+    y_copy(z, PIECES - 1).wait_send()
+    for slot in range(3):
+        x_copy(tp, slot, core_id, True).wait_send()
+    for distance in range(Z_SIZE - 1):
+        for part in range(PIECES + 1):
+            @pl.when((z < Z_SIZE - 1) & (z >= distance))
+            def _():
+                z_copy(z - distance, distance, part, True).wait_send()
+
+            @pl.when((z > 0) & (z + distance < Z_SIZE))
+            def _():
+                z_copy(z + distance, distance, part, False).wait_send()
+    for copy in keep:
+        copy.wait()
+
+
+def gather_inputs(normed, w_query, key_matrix, value_matrix):
+    depth = w_query.shape[0]
+    width = w_query.shape[1] + 2 * key_matrix.shape[1]
+    tokens_own, model = normed.shape
+    y_slots = Z_SIZE * (PIECES - 1) + 1
+    z_slots = (Z_SIZE - 1) * (PIECES + 1)
+    dma = pltpu.SemaphoreType.DMA
+    return pl.pallas_call(
+        gather_kernel,
+        out_shape=(
+            jax.ShapeDtypeStruct((4 * tokens_own, model), jnp.bfloat16),
+            jax.ShapeDtypeStruct((2 * Z_SIZE * depth, width), jnp.bfloat16),
+        ),
+        in_specs=[pl.BlockSpec(memory_space=pl.ANY)] * 4,
+        out_specs=(pl.BlockSpec(memory_space=pl.ANY),) * 2,
+        scratch_shapes=[
+            pltpu.VMEM((tokens_own, model), jnp.bfloat16),
+            pltpu.VMEM((depth, width), jnp.bfloat16),
+            dma((4,)), dma((3,)), dma((3,)), dma((y_slots,)), dma((y_slots,)),
+            dma((z_slots,)), dma((z_slots,)), dma((z_slots,)), dma((z_slots,)),
+        ],
+        compiler_params=pltpu.CompilerParams(collective_id=0, has_side_effects=True),
+        name="gather_inputs",
+    )(normed, w_query, key_matrix, value_matrix)
 
 
 def attend(query_matrix, projected_keys, projected_values, query_offsets, key_offsets, key_valid):
@@ -72,19 +280,27 @@
     gain_key,
     gain_post,
 ):
-    gathered = lax.all_gather(tokens, "tp", axis=0, tiled=True)
-    normalized_rows = row_norm(gathered.astype(jnp.float32), gain_in).astype(jnp.bfloat16)
+    normed = row_norm(tokens.astype(jnp.float32), gain_in).astype(jnp.bfloat16)
+    if lax.axis_size("ctx") == 2 * Z_SIZE and lax.axis_size("tp") == 4:
+        normalized_rows, weights_in = gather_inputs(normed, w_query, key_matrix, value_matrix)
+        normalized_rows, weights_in, w_out = lax.optimization_barrier(
+            (normalized_rows, weights_in, w_out)
+        )
+    else:
+        normalized_rows = lax.all_gather(normed, "tp", axis=0, tiled=True)
+        weights_in = lax.all_gather(
+            jnp.concatenate([w_query, key_matrix, value_matrix], axis=1), "ctx", axis=0, tiled=True
+        )
+    w_out_full = lax.all_gather(w_out, "ctx", axis=1, tiled=True)
     row_count = normalized_rows.shape[0]
     block_start = lax.axis_index("ctx") * row_count
     offsets_all = positions - positions[0]
     query_offsets = lax.dynamic_slice_in_dim(offsets_all, block_start, row_count, 0)
-
-    def add_rows(weight_rows):
-        return jnp.dot(normalized_rows, weight_rows, preferred_element_type=jnp.float32)
-
-    query_raw = add_rows(lax.all_gather(w_query, "ctx", axis=0, tiled=True))
-    unnormed_keys = add_rows(lax.all_gather(key_matrix, "ctx", axis=0, tiled=True))
-    value_raw = add_rows(lax.all_gather(value_matrix, "ctx", axis=0, tiled=True))
+    raw = jnp.dot(normalized_rows, weights_in, preferred_element_type=jnp.float32)
+    query_width, key_width = w_query.shape[1], key_matrix.shape[1]
+    query_raw = raw[:, :query_width]
+    unnormed_keys = raw[:, query_width : query_width + key_width]
+    value_raw = raw[:, query_width + key_width :]
     key_heads = key_matrix.shape[1] // HEAD_SIZE
     projected_keys = rotate(
         row_norm(unnormed_keys.reshape(row_count, key_heads, HEAD_SIZE), gain_key), query_offsets
@@ -117,7 +333,7 @@
     )
     projected = jnp.dot(
         attended,
-        lax.all_gather(w_out, "ctx", axis=1, tiled=True),
+        w_out_full,
         preferred_element_type=jnp.float32,
     )
     summed = lax.psum_scatter(

time: 435 us -> 302 us (0.69)
  waiting for transfers between devices: 353 us -> 104 us
  Pallas kernels: 0 us -> 110 us
  matrix products: 39.2 us -> 30.7 us
  starting transfers between devices: 11.8 us -> 20.1 us
    all_gather x5 -> x1, waiting for transfers between devices: 276 us -> 28.4 us  [shards(): w_out_full = lax.all_gather(w_out, 'ctx', axis=1, tiled=True)]
    pallas_call x0 -> x1, Pallas kernels: none -> 110 us  [gather_inputs(): pl.pallas_call(gather_kernel, out_shape=(jax.ShapeDtypeStruct((4 * tokens...]
    dot_general x4 -> x2, matrix products: 26.3 us -> 17.7 us  [the longest x1 10.2 us: shards(): jnp.dot(normalized_rows, weights_in, preferred_element_type=jnp.float32)]
    ppermute x2, starting transfers between devices: 11.6 us -> 20 us  [shifted(): lax.ppermute(value, axis, [(source, source + steps) for source in range(l...]
  transfers between devices with their start and end apart: 8 -> 4, of which waited for: 8 -> 4; matrix products, arithmetic and copies ran while one was open for 10% -> 12% of each run, Pallas kernels for 0% -> 0%
where the time goes in v1:
time: 302 us
  Pallas kernels  110 us (36%)
  waiting for transfers between devices  104 us (34%)
  matrix products  30.7 us (10%)
  starting transfers between devices  20.1 us (7%)
  other arithmetic  17.6 us (6%)
  between operations  13.6 us (5%)
  local copies, waits for them, and re-layouts  5.81 us (2%)
    pallas_call x1, Pallas kernels, gather_inputs(): pl.pallas_call(gather_kernel, out_shape=(jax.ShapeDtypeStruct((4 * tokens...  110 us
    reduce_scatter x1, waiting for transfers between devices, shards(): lax.psum_scatter(projected.astype(jnp.bfloat16), 'tp', scatter_dimension=...  51.5 us
    all_gather x1, waiting for transfers between devices, shards(): w_out_full = lax.all_gather(w_out, 'ctx', axis=1, tiled=True)  28.4 us
    ppermute x2, waiting for transfers between devices, shifted(): lax.ppermute(value, axis, [(source, source + steps) for source in range(l...  23.6 us
    ppermute x2, starting transfers between devices, shifted(): lax.ppermute(value, axis, [(source, source + steps) for source in range(l...  20 us
    dot_general x1, matrix products, shards(): jnp.dot(normalized_rows, weights_in, preferred_element_type=jnp.float32)  10.2 us
    sub x1, matrix products, attend(): weights = jnp.where(allowed[None, None], jnp.exp(scores - row_max), 0.0)  9.14 us
    dot_general x1, matrix products, shards(): jnp.dot(attended, w_out_full, preferred_element_type=jnp.float32)  7.46 us
  transfers between devices with their start and end apart: 4, of which 4 were waited for; matrix products, arithmetic and copies ran while one was open for 12% of the time, Pallas kernels for 0%

profile of v1, /device:TPU:0, one launch (start us, length us, event | category | flops | bytes accessed | tf_op | source)
XLA Modules:
  0.0 301.6 jit_solution(12303072293458800752)
XLA Ops:
  6.5 1.7 fusion.11
  8.2 2.8 fusion.13.x_ref
  11.0 110.2 %gather_inputs.1 = (bf16[512,5376]{1,0:T(8,128)(2,1)}, bf16[5376,1024]{1,0:T(8,128)(2,1)}) custom-call(bf16[128,5376]{1,0:T(8,128)(2,1)} %fusion.13.x_ref, bf16[672,512]{1,0:T(8,128)(2,1)} %q_ref.1, bf16[672,256]{1,0:T(8,128)(2,1)} %k_ref.1, bf16[672,256]{1,0:T(8,128)(2,1)} %v_ref.1), custom_call_target="tpu_custom_call" | custom-call | tf_op jit(solution)/shard_map/gather_inputs/pallas_call | solution.py:234
  121.3 10.2 %fusion.39 = f32[512,1024]{1,0:T(8,128)S(1)} fusion(bf16[512,5376]{1,0:T(8,128)(2,1)} %get-tuple-element.12, bf16[5376,1024]{1,0:T(8,128)(2,1)} %get-tuple-element.13), kind=kOutput, calls=%fused_computation.65 | convolution fusion | flops 5637144576 | bytes 18612224 | tf_op jit(solution)/shard_map/dot_general | solution.py:299
  131.7 1.2 copy-done.1
  135.3 1.0 multiply_cosine_fusion
  136.8 1.0 pad_maximum_fusion
  137.7 4.3 %collective-permute-start = (bf16[2,512,2,128]{3,1,2,0:T(8,128)(2,1)}, bf16[2,512,2,128]{3,1,2,0:T(8,128)(2,1)}, u32[]{:S(2)}, u32[]{:S(2)}) collective-permute-start(bf16[2,512,2,128]{3,1,2,0:T(8,128)(2,1)} %pad_maximum_fusion), channel_id=1, source_target_pairs={{0,4},{4,8},{8,12},{12,16},{16,20},{20,24},{24,28},{1,5},{5,9},{9,... | collective-permute-start | bytes 1572872 | tf_op jit(solution)/shard_map/ppermute | solution.py:20
  142.1 1.3 slice.47
  145.2 0.8 subtract_convert_fusion
  146.1 6.1 %collective-permute-done = bf16[2,512,2,128]{3,1,2,0:T(8,128)(2,1)} collective-permute-done((bf16[2,512,2,128]{3,1,2,0:T(8,128)(2,1)}, bf16[2,512,2,128]{3,1,2,0:T(8,128)(2,1)}, u32[]{:S(2)}, u32[]{:S(2)}) %collective-permute-start) | collective-permute-done | bytes 524320 | tf_op jit(solution)/shard_map/ppermute | solution.py:20
  152.2 15.7 %collective-permute-start.1 = (bf16[2,512,2,128]{3,1,2,0:T(8,128)(2,1)}, bf16[2,512,2,128]{3,1,2,0:T(8,128)(2,1)S(1)}, u32[]{:S(2)}, u32[]{:S(2)}) collective-permute-start(bf16[2,512,2,128]{3,1,2,0:T(8,128)(2,1)} %collective-permute-done), channel_id=1, source_target_pairs={{0,4},{4,8},{8,12},{12,16},{16,20},{20,24},{24,28},{1,5},{5,9},{9,... | collective-permute-start | bytes 1572872 | tf_op jit(solution)/shard_map/ppermute | solution.py:20
  167.9 0.9 copy.37
  168.7 0.9 copy.38
  169.6 1.2 fusion.8
  170.8 17.5 %collective-permute-done.1 = bf16[2,512,2,128]{3,1,2,0:T(8,128)(2,1)S(1)} collective-permute-done((bf16[2,512,2,128]{3,1,2,0:T(8,128)(2,1)}, bf16[2,512,2,128]{3,1,2,0:T(8,128)(2,1)S(1)}, u32[]{:S(2)}, u32[]{:S(2)}) %collective-permute-start.1) | collective-permute-done | bytes 524320 | tf_op jit(solution)/shard_map/ppermute | solution.py:20
  188.3 1.2 maximum_maximum_fusion
  189.6 9.1 %fusion.38 = (f32[2,2,512]{2,1,0:T(2,128)S(1)}, bf16[2,2,512,1536]{2,3,1,0:T(8,128)(2,1)}) fusion(pred[512,1536]{0,1:T(8,128)(4,1)S(1)} %fusion.8, bf16[2,1536,2,128]{3,1,2,0:T(8,128)(2,1)S(1)} %maximum_maximum_fusion, bf16[512,2,2,64]{3,0,2,1:T(8,128)(2,1)} %bitcast.64, bf16[512,2,2,64]{3,0,2,1:T(8,128)(2,1)} %bitcast.63), kind=kOutput, calls=%fused_computation.64 | convolution fusion | flops 825230848 | bytes 9183232 | tf_op jit(solution)/shard_map/sub | solution.py:261
  198.7 3.8 %fusion.23 = bf16[512,2,2,128]{0,3,2,1:T(8,128)(2,1)S(1)} fusion(bf16[2,2,512,1536]{2,3,1,0:T(8,128)(2,1)} %get-tuple-element.26, bf16[2,1536,2,128]{3,1,2,0:T(8,128)(2,1)S(1)} %maximum_maximum_fusion, f32[512,2,2]{0,2,1:T(2,128)S(1)} %bitcast.66), kind=kOutput, calls=%fused_computation.29 | convolution fusion | flops 805830656 | bytes 7610368 | tf_op jit(solution)/shard_map/kgqs,skd->qkgd/dot_general | solution.py:264
  202.6 28.4 %all-gather.2.cloned.1.call-done = bf16[512,5376]{0,1:T(8,128)(2,1)} async-done(((bf16[512,672]{0,1:T(8,128)(2,1)}), bf16[512,5376]{0,1:T(8,128)(2,1)}) %all-gather.2.cloned.1.call-update) | async-done | bytes 5505040 | tf_op jit(solution)/shard_map/all_gather | solution.py:294
  231.0 7.5 %convolution_convert_fusion = bf16[512,5376]{1,0:T(8,128)(2,1)} fusion(bf16[512,512]{0,1:T(8,128)(2,1)S(1)} %bitcast.65, bf16[512,5376]{0,1:T(8,128)(2,1)} %all-gather.2.cloned.1.call-done), kind=kOutput, calls=%fused_computation.4 | convolution fusion | flops 2821324800 | bytes 11534336 | tf_op jit(solution)/shard_map/dot_general | solution.py:334
  238.5 51.5 %reduce-scatter.2.cloned.1.call-done = bf16[128,5376]{1,0:T(8,128)(2,1)} async-done(((bf16[512,5376]{1,0:T(8,128)(2,1)}), bf16[128,5376]{1,0:T(8,128)(2,1)}) %reduce-scatter.2.cloned.1.call-update) | async-done | bytes 1376272 | tf_op jit(solution)/shard_map/reduce_scatter | solution.py:339
  290.0 1.7 fusion.9
  291.7 3.0 fusion.14
  (37 shorter events, 4.9 us)
Async XLA Ops:
  6.5 224.5 %all-gather.2.cloned.1.call-start = ((), (), s32[]{:S(2)}) async-start(), calls=%async_computation.1 | async-start | bytes 6193152 | tf_op jit(solution)/shard_map/all_gather | solution.py:294
  121.2 168.8 %reduce-scatter.2.cloned.1.call-start = ((), (), s32[]{:S(2)}) async-start(), calls=%async_computation.2 | async-start | bytes 6881280 | tf_op jit(solution)/shard_map/reduce_scatter | solution.py:339
  131.5 1.3 copy-start.1
  131.5 2.3 copy-start.3
  131.6 4.7 %copy-start.4 = (f32[128]{0:T(128)S(1)}, f32[128]{0:T(128)}, u32[]{:S(2)}) copy-start(f32[128]{0:T(128)} %param.18) | copy-start | bytes 1540
  137.7 6.8 %copy-start.5 = (f32[128]{0:T(128)S(1)}, f32[128]{0:T(128)}, u32[]{:S(2)}) copy-start(f32[128]{0:T(128)} %param.17) | copy-start | bytes 1540
  137.7 14.5 %collective-permute-start = (bf16[2,512,2,128]{3,1,2,0:T(8,128)(2,1)}, bf16[2,512,2,128]{3,1,2,0:T(8,128)(2,1)}, u32[]{:S(2)}, u32[]{:S(2)}) collective-permute-start(bf16[2,512,2,128]{3,1,2,0:T(8,128)(2,1)} %pad_maximum_fusion), channel_id=1, source_target_pairs={{0,4},{4,8},{8,12},{12,16},{16,20},{20,24},{24,28},{1,5},{5,9},{9,... | collective-permute-start | bytes 1572872 | tf_op jit(solution)/shard_map/ppermute | solution.py:20
  152.2 36.2 %collective-permute-start.1 = (bf16[2,512,2,128]{3,1,2,0:T(8,128)(2,1)}, bf16[2,512,2,128]{3,1,2,0:T(8,128)(2,1)S(1)}, u32[]{:S(2)}, u32[]{:S(2)}) collective-permute-start(bf16[2,512,2,128]{3,1,2,0:T(8,128)(2,1)} %collective-permute-done), channel_id=1, source_target_pairs={{0,4},{4,8},{8,12},{12,16},{16,20},{20,24},{24,28},{1,5},{5,9},{9,... | collective-permute-start | bytes 1572872 | tf_op jit(solution)/shard_map/ppermute | solution.py:20
  238.5 53.2 %copy-start = (bf16[128,5376]{1,0:T(8,128)(2,1)S(1)}, bf16[128,5376]{1,0:T(8,128)(2,1)}, u32[]{:S(2)}) copy-start(bf16[128,5376]{1,0:T(8,128)(2,1)} %param.10) | copy-start | bytes 4128772
  238.5 53.3 %copy-start.2 = (f32[5376]{0:T(1024)S(1)}, f32[5376]{0:T(1024)}, u32[]{:S(2)}) copy-start(f32[5376]{0:T(1024)} %param.19) | copy-start | bytes 64516
Sparse Core Ops, SparseCore 0:
  121.4 109.6 all-gather.1
  238.6 51.3 reduce-scatter.1

commit v2 on v0

--- a/solution.py
+++ b/solution.py
@@ -1,6 +1,8 @@
 import jax
 import jax.numpy as jnp
 from jax import lax
+from jax.experimental import pallas as pl
+from jax.experimental.pallas import tpu as pltpu
 from jax.sharding import PartitionSpec as P
 
 HEAD_SIZE = 128
@@ -40,6 +42,372 @@
         ],
         axis=-1,
     )
+
+
+Z_SIZE = 4
+TILE = 16
+CUTS = (0, 11, 23, 35, 42)
+PIECES = len(CUTS) - 1
+ROW_STEP = 336
+MESH = pl.DeviceIdType.MESH
+
+
+def remote(source, target, send, recv, device):
+    return pltpu.make_async_remote_copy(
+        src_ref=source, dst_ref=target, send_sem=send, recv_sem=recv,
+        device_id=device, device_id_type=MESH,
+    )
+
+
+class Places:
+    def __init__(self):
+        self.ctx = lax.axis_index("ctx")
+        self.tp = lax.axis_index("tp")
+        self.z, self.y = self.ctx // 2, self.ctx % 2
+        self.y_other = 1 - self.y
+        self.x_peer = (self.tp + 2) % 4
+        self.y_id = (self.z * 2 + self.y_other, self.tp)
+        self.up_id = (self.ctx + 2, self.tp)
+        self.down_id = (self.ctx - 2, self.tp)
+        self.core_id = (self.ctx, self.tp + 1 - 2 * (self.tp % 2))
+        self.x_id = (self.ctx, self.x_peer)
+
+    def greet(self):
+        barrier = pltpu.get_barrier_semaphore()
+
+        def signal(target):
+            pl.semaphore_signal(barrier, inc=1, device_id=target, device_id_type=MESH)
+
+        signal(self.y_id)
+        signal(self.core_id)
+        signal(self.x_id)
+
+        @pl.when(self.z < Z_SIZE - 1)
+        def _():
+            signal(self.up_id)
+
+        @pl.when(self.z > 0)
+        def _():
+            signal(self.down_id)
+
+    def meet(self):
+        z = self.z
+        pl.semaphore_wait(pltpu.get_barrier_semaphore(), 4 + ((z + 1) // 2) % 2)
+
+
+class Gather:
+    def __init__(self, places, own, whole, depth, sems):
+        self.at, self.own, self.whole, self.depth = places, own, whole, depth
+        self.y_send, self.y_recv, self.up_send, self.down_send, self.below, self.above = sems
+
+    def rows(self, owner, part):
+        start, stop = CUTS[part] * TILE, CUTS[part + 1] * TILE
+        return self.whole.at[
+            pl.ds(pl.multiple_of(owner * self.depth + start, TILE), stop - start)
+        ]
+
+    def own_part(self, part):
+        return self.own(CUTS[part] * TILE, (CUTS[part + 1] - CUTS[part]) * TILE)
+
+    def place(self, plane, part):
+        if part < PIECES:
+            return self.rows(plane * 2 + self.at.y, part)
+        return self.rows(plane * 2 + self.at.y_other, PIECES - 1)
+
+    def y_copy(self, plane, part, own=False):
+        target = self.rows(plane * 2 + self.at.y, part)
+        slot = Z_SIZE * (PIECES - 1) if part == PIECES - 1 else plane * (PIECES - 1) + part
+        source = self.own_part(part) if own else target
+        return remote(source, target, self.y_send.at[slot], self.y_recv.at[slot], self.at.y_id)
+
+    def z_copy(self, plane, distance, part, upward):
+        target = self.place(plane, part)
+        source = self.own_part(part) if distance == 0 and part < PIECES else target
+        slot = distance * (PIECES + 1) + part
+        if upward:
+            return remote(
+                source, target, self.up_send.at[slot], self.below.at[slot], self.at.up_id
+            )
+        return remote(
+            source, target, self.down_send.at[slot], self.above.at[slot], self.at.down_id
+        )
+
+    def send_z(self, part):
+        z = self.at.z
+
+        @pl.when(z < Z_SIZE - 1)
+        def _():
+            self.z_copy(z, 0, part, True).start()
+
+        @pl.when(z > 0)
+        def _():
+            self.z_copy(z, 0, part, False).start()
+
+    def start(self):
+        z = self.at.z
+        self.y_copy(z, PIECES - 1, own=True).start()
+        for part in range(PIECES - 1):
+            self.send_z(part)
+            self.y_copy(z, part, own=True).start()
+        self.send_z(PIECES - 1)
+
+    def cross(self):
+        self.y_copy(self.at.z, PIECES - 1).wait_recv()
+        self.send_z(PIECES)
+
+    def relay(self, distance, part):
+        z = self.at.z
+
+        @pl.when(z >= distance)
+        def _():
+            self.z_copy(z - distance, distance - 1, part, True).wait_recv()
+            if distance < Z_SIZE - 1:
+                @pl.when(z < Z_SIZE - 1)
+                def _():
+                    self.z_copy(z - distance, distance, part, True).start()
+            if part < PIECES - 1:
+                self.y_copy(z - distance, part).start()
+
+        @pl.when(z + distance < Z_SIZE)
+        def _():
+            self.z_copy(z + distance, distance - 1, part, False).wait_recv()
+            if distance < Z_SIZE - 1:
+                @pl.when(z > 0)
+                def _():
+                    self.z_copy(z + distance, distance, part, False).start()
+            if part < PIECES - 1:
+                self.y_copy(z + distance, part).start()
+
+    def wait_plane(self, plane):
+        for part in range(PIECES - 1):
+            self.y_copy(plane, part).wait_recv()
+
+    def drain(self):
+        z = self.at.z
+        for plane in range(Z_SIZE):
+            for part in range(PIECES - 1):
+                self.y_copy(plane, part).wait_send()
+        self.y_copy(z, PIECES - 1).wait_send()
+        for distance in range(Z_SIZE - 1):
+            for part in range(PIECES + 1):
+                @pl.when((z < Z_SIZE - 1) & (z >= distance))
+                def _():
+                    self.z_copy(z - distance, distance, part, True).wait_send()
+
+                @pl.when((z > 0) & (z + distance < Z_SIZE))
+                def _():
+                    self.z_copy(z + distance, distance, part, False).wait_send()
+
+
+def gather_semaphores():
+    y_slots = Z_SIZE * (PIECES - 1) + 1
+    z_slots = (Z_SIZE - 1) * (PIECES + 1)
+    return [pltpu.SemaphoreType.DMA((n,)) for n in (y_slots, y_slots) + (z_slots,) * 4]
+
+
+def gather_kernel(
+    x_ref, q_ref, k_ref, v_ref, xg_ref, wg_ref, xs, ws, stage_sem, x_send, x_recv, *sems
+):
+    at = Places()
+    depth, tokens_own = q_ref.shape[0], x_ref.shape[0]
+    q_width, k_width = q_ref.shape[1], k_ref.shape[1]
+    at.greet()
+    loads = [
+        pltpu.make_async_copy(q_ref, ws.at[:, pl.ds(0, q_width)], stage_sem.at[0]),
+        pltpu.make_async_copy(k_ref, ws.at[:, pl.ds(q_width, k_width)], stage_sem.at[1]),
+        pltpu.make_async_copy(v_ref, ws.at[:, pl.ds(q_width + k_width, k_width)], stage_sem.at[2]),
+        pltpu.make_async_copy(x_ref, xs, stage_sem.at[3]),
+    ]
+    for copy in loads:
+        copy.start()
+    for copy in loads:
+        copy.wait()
+    at.meet()
+    gather = Gather(at, lambda begin, size: ws.at[pl.ds(begin, size)], wg_ref, depth, sems)
+
+    def token_rows(owner):
+        return xg_ref.at[pl.ds(pl.multiple_of(owner * tokens_own, TILE), tokens_own)]
+
+    def x_copy(owner, slot, device, own):
+        target = token_rows(owner)
+        return remote(xs if own else target, target, x_send.at[slot], x_recv.at[slot], device)
+
+    x_copy(at.tp, 0, at.x_id, True).start()
+    x_copy(at.tp, 1, at.core_id, True).start()
+    gather.start()
+    keep = [
+        pltpu.make_async_copy(
+            ws, wg_ref.at[pl.ds(pl.multiple_of(at.ctx * depth, TILE), depth)], stage_sem.at[0]
+        ),
+        pltpu.make_async_copy(xs, token_rows(at.tp), stage_sem.at[3]),
+    ]
+    for copy in keep:
+        copy.start()
+    gather.cross()
+    for distance in range(1, Z_SIZE):
+        for part in range(PIECES + 1):
+            gather.relay(distance, part)
+        if distance == 1:
+            x_copy(at.x_peer, 0, at.x_id, False).wait_recv()
+            x_copy(at.x_peer, 2, at.core_id, False).start()
+    x_copy(at.tp, 1, at.core_id, False).wait_recv()
+    x_copy(at.x_peer, 2, at.core_id, False).wait_recv()
+    for plane in range(Z_SIZE):
+        gather.wait_plane(plane)
+    gather.drain()
+    for slot in range(3):
+        x_copy(at.tp, slot, at.core_id, True).wait_send()
+    for copy in keep:
+        copy.wait()
+
+
+def gather_inputs(normed, w_query, key_matrix, value_matrix):
+    depth = w_query.shape[0]
+    width = w_query.shape[1] + 2 * key_matrix.shape[1]
+    tokens_own, model = normed.shape
+    dma = pltpu.SemaphoreType.DMA
+    return pl.pallas_call(
+        gather_kernel,
+        out_shape=(
+            jax.ShapeDtypeStruct((4 * tokens_own, model), jnp.bfloat16),
+            jax.ShapeDtypeStruct((2 * Z_SIZE * depth, width), jnp.bfloat16),
+        ),
+        in_specs=[pl.BlockSpec(memory_space=pl.ANY)] * 4,
+        out_specs=(pl.BlockSpec(memory_space=pl.ANY),) * 2,
+        scratch_shapes=[
+            pltpu.VMEM((tokens_own, model), jnp.bfloat16),
+            pltpu.VMEM((depth, width), jnp.bfloat16),
+            dma((4,)), dma((3,)), dma((3,)), *gather_semaphores(),
+        ],
+        compiler_params=pltpu.CompilerParams(collective_id=0, has_side_effects=True),
+        name="gather_inputs",
+    )(normed, w_query, key_matrix, value_matrix)
+
+
+def project_kernel(
+    w_ref, mine_ref, peer_ref, out_ref,
+    whole, kept, sent_core, got_core, sent_x, got_x,
+    stage_sem, core_send, core_recv, x_send, x_recv, *sems,
+):
+    at = Places()
+    depth = w_ref.shape[0]
+    tokens_own = out_ref.shape[1]
+    plane_rows = 2 * depth
+    z = at.z
+    at.greet()
+
+    def own_rows(begin, size):
+        return whole.at[pl.ds(pl.multiple_of(at.ctx * depth + begin, TILE), size)]
+
+    load = pltpu.make_async_copy(w_ref, own_rows(0, depth), stage_sem)
+    load.start()
+    load.wait()
+    at.meet()
+    gather = Gather(at, own_rows, whole, depth, sems)
+    planes = [z, z + 1 - 2 * (z % 2), (z + 2) % 4, 3 - z]
+    x_mine = at.tp // 2
+    mine_columns = pl.ds(pl.multiple_of(x_mine * tokens_own, 128), tokens_own)
+    other_columns = pl.ds(pl.multiple_of((1 - x_mine) * tokens_own, 128), tokens_own)
+
+    def core_copy(step):
+        return remote(
+            sent_core.at[step], got_core.at[step], core_send.at[step], core_recv.at[step],
+            at.core_id,
+        )
+
+    def x_copy(step):
+        return remote(
+            sent_x.at[step], got_x.at[step], x_send.at[step], x_recv.at[step], at.x_id
+        )
+
+    def product(rows, tokens):
+        return lax.dot_general(
+            rows, tokens, (((1,), (1,)), ((), ())), preferred_element_type=jnp.float32
+        )
+
+    def project(step):
+        first = planes[step] * plane_rows
+
+        @pl.loop(0, plane_rows // ROW_STEP)
+        def _(block):
+            rows = whole[pl.ds(pl.multiple_of(first + block * ROW_STEP, TILE), ROW_STEP), :]
+            here = pl.ds(pl.multiple_of(block * ROW_STEP, TILE), ROW_STEP)
+            sent_core[step, here, :] = product(rows, peer_ref[...]).astype(jnp.bfloat16)
+            kept[step, here, :] = product(rows, mine_ref[...])
+
+        core_copy(step).start()
+
+    def pass_on(step):
+        core_copy(step).wait_recv()
+
+        @pl.loop(0, plane_rows // ROW_STEP)
+        def _(block):
+            here = pl.ds(pl.multiple_of(block * ROW_STEP, TILE), ROW_STEP)
+            total = kept[step, here, other_columns] + got_core[step, here, other_columns].astype(
+                jnp.float32
+            )
+            sent_x[step, here, :] = total.astype(jnp.bfloat16)
+
+        x_copy(step).start()
+
+    def finish(step):
+        x_copy(step).wait_recv()
+        first = planes[step] * plane_rows
+
+        @pl.loop(0, plane_rows // ROW_STEP)
+        def _(block):
+            here = pl.ds(pl.multiple_of(block * ROW_STEP, TILE), ROW_STEP)
+            there = pl.ds(pl.multiple_of(first + block * ROW_STEP, TILE), ROW_STEP)
+            out_ref[there, :] = (
+                kept[step, here, mine_columns]
+                + got_core[step, here, mine_columns].astype(jnp.float32)
+                + got_x[step, here, :].astype(jnp.float32)
+            )
+
+    gather.start()
+    gather.cross()
+    gather.wait_plane(z)
+    project(0)
+    for distance in range(1, Z_SIZE):
+        for part in range(PIECES + 1):
+            gather.relay(distance, part)
+            if part == 1:
+                pass_on(distance - 1)
+        gather.wait_plane(planes[distance])
+        project(distance)
+    pass_on(Z_SIZE - 1)
+    for step in range(Z_SIZE):
+        finish(step)
+    gather.drain()
+    for step in range(Z_SIZE):
+        core_copy(step).wait_send()
+        x_copy(step).wait_send()
+
+
+def project_out(w_rows, mine, peer):
+    depth, heads = w_rows.shape
+    tokens_own = mine.shape[0] // 2
+    plane_rows = 2 * depth
+    bf16, dma = jnp.bfloat16, pltpu.SemaphoreType.DMA
+    vmem = pl.BlockSpec(memory_space=pltpu.VMEM)
+    return pl.pallas_call(
+        project_kernel,
+        out_shape=jax.ShapeDtypeStruct((Z_SIZE * plane_rows, tokens_own), jnp.float32),
+        in_specs=[pl.BlockSpec(memory_space=pl.ANY), vmem, vmem],
+        out_specs=vmem,
+        scratch_shapes=[
+            pltpu.VMEM((Z_SIZE * plane_rows, heads), bf16),
+            pltpu.VMEM((Z_SIZE, plane_rows, 2 * tokens_own), jnp.float32),
+            pltpu.VMEM((Z_SIZE, plane_rows, 2 * tokens_own), bf16),
+            pltpu.VMEM((Z_SIZE, plane_rows, 2 * tokens_own), bf16),
+            pltpu.VMEM((Z_SIZE, plane_rows, tokens_own), bf16),
+            pltpu.VMEM((Z_SIZE, plane_rows, tokens_own), bf16),
+            dma, dma((Z_SIZE,)), dma((Z_SIZE,)), dma((Z_SIZE,)), dma((Z_SIZE,)),
+            *gather_semaphores(),
+        ],
+        compiler_params=pltpu.CompilerParams(collective_id=1, has_side_effects=True),
+        name="project_out",
+    )(w_rows, mine, peer)
 
 
 def attend(query_matrix, projected_keys, projected_values, query_offsets, key_offsets, key_valid):
@@ -72,19 +440,28 @@
     gain_key,
     gain_post,
 ):
-    gathered = lax.all_gather(tokens, "tp", axis=0, tiled=True)
-    normalized_rows = row_norm(gathered.astype(jnp.float32), gain_in).astype(jnp.bfloat16)
+    normed = row_norm(tokens.astype(jnp.float32), gain_in).astype(jnp.bfloat16)
+    kernels = lax.axis_size("ctx") == 2 * Z_SIZE and lax.axis_size("tp") == 4
+    if kernels:
+        normalized_rows, weights_in = gather_inputs(normed, w_query, key_matrix, value_matrix)
+    else:
+        normalized_rows = lax.all_gather(normed, "tp", axis=0, tiled=True)
+        weights_in = lax.all_gather(
+            jnp.concatenate([w_query, key_matrix, value_matrix], axis=1), "ctx", axis=0, tiled=True
+        )
     row_count = normalized_rows.shape[0]
     block_start = lax.axis_index("ctx") * row_count
     offsets_all = positions - positions[0]
     query_offsets = lax.dynamic_slice_in_dim(offsets_all, block_start, row_count, 0)
-
-    def add_rows(weight_rows):
-        return jnp.dot(normalized_rows, weight_rows, preferred_element_type=jnp.float32)
-
-    query_raw = add_rows(lax.all_gather(w_query, "ctx", axis=0, tiled=True))
-    unnormed_keys = add_rows(lax.all_gather(key_matrix, "ctx", axis=0, tiled=True))
-    value_raw = add_rows(lax.all_gather(value_matrix, "ctx", axis=0, tiled=True))
+    query_width, key_width = w_query.shape[1], key_matrix.shape[1]
+
+    def add_rows(weights):
+        return jnp.dot(normalized_rows, weights, preferred_element_type=jnp.float32)
+
+    key_value_raw = add_rows(weights_in[:, query_width:])
+    query_raw = add_rows(weights_in[:, :query_width])
+    unnormed_keys = key_value_raw[:, :key_width]
+    value_raw = key_value_raw[:, key_width:]
     key_heads = key_matrix.shape[1] // HEAD_SIZE
     projected_keys = rotate(
         row_norm(unnormed_keys.reshape(row_count, key_heads, HEAD_SIZE), gain_key), query_offsets
@@ -92,11 +469,7 @@
     projected_values = value_raw.astype(jnp.bfloat16).reshape(row_count, key_heads, HEAD_SIZE)
     own_pair = jnp.stack([projected_keys, projected_values])
     window_blocks = LOOKBACK_WINDOW // row_count
-    earlier = []
-    carried = own_pair
-    for relay_step in range(window_blocks):
-        carried = shifted(carried, "ctx", 1)
-        earlier.insert(0, carried)
+    earlier = [shifted(own_pair, "ctx", steps) for steps in range(window_blocks, 0, -1)]
     window_pair = jnp.concatenate(earlier + [own_pair], axis=1)
     query_heads = w_query.shape[1] // HEAD_SIZE
     query_matrix = rotate(
@@ -115,14 +488,22 @@
     attended = attend(
         query_matrix, window_pair[0], window_pair[1], query_offsets, key_offsets, key_valid
     )
-    projected = jnp.dot(
-        attended,
-        lax.all_gather(w_out, "ctx", axis=1, tiled=True),
-        preferred_element_type=jnp.float32,
-    )
-    summed = lax.psum_scatter(
-        projected.astype(jnp.bfloat16), "tp", scatter_dimension=0, tiled=True
-    ).astype(jnp.float32)
+    if kernels:
+        by_core = attended.reshape(2, 2, row_count // 4, attended.shape[1])
+        core = lax.axis_index("tp") % 2
+        mine = lax.dynamic_index_in_dim(by_core, core, 1, keepdims=False)
+        peer = lax.dynamic_index_in_dim(by_core, 1 - core, 1, keepdims=False)
+        flat = (row_count // 2, attended.shape[1])
+        summed = project_out(w_out.T, mine.reshape(flat), peer.reshape(flat)).T
+    else:
+        projected = jnp.dot(
+            attended,
+            lax.all_gather(w_out, "ctx", axis=1, tiled=True),
+            preferred_element_type=jnp.float32,
+        )
+        summed = lax.psum_scatter(
+            projected.astype(jnp.bfloat16), "tp", scatter_dimension=0, tiled=True
+        ).astype(jnp.float32)
     return (tokens.astype(jnp.float32) + row_norm(summed, gain_post)).astype(jnp.bfloat16)
 
 

time: 435 us -> 262 us (0.60)
  waiting for transfers between devices: 353 us -> 0.01 us
  Pallas kernels: 0 us -> 196 us
  between operations: 13.7 us -> 0.28 us
  matrix products: 39.2 us -> 28.2 us
  local copies, waits for them, and re-layouts: 3.21 us -> 11.5 us
  starting transfers between devices: 11.8 us -> 6.24 us
    all_gather x5 -> x0, waiting for transfers between devices: 276 us -> none  [the longest x1 66.7 us: shards(): lax.all_gather(w_out, 'ctx', axis=1, tiled=True)]
    pallas_call x0 -> x2, Pallas kernels: none -> 196 us  [the longest x1 110 us: gather_inputs(): pl.pallas_call(gather_kernel, out_shape=(jax.ShapeDtypeStruct((4 * tokens...]
    reduce_scatter x1 -> x0, waiting for transfers between devices: 51.3 us -> none  [shards(): lax.psum_scatter(projected.astype(jnp.bfloat16), 'tp', scatter_dimension=...]
    ppermute x2, waiting for transfers between devices: 22 us -> 0.01 us  [shifted(): lax.ppermute(value, axis, [(source, source + steps) for source in range(l...]
    dot_general x4 -> x2, matrix products: 26.3 us -> 13.5 us  [add_rows(): return jnp.dot(normalized_rows, weights, preferred_element_type=jnp.float32)]
    ppermute x2, starting transfers between devices: 11.6 us -> 6.24 us  [shifted(): lax.ppermute(value, axis, [(source, source + steps) for source in range(l...]
    unnamed x12 -> x17, local copies, waits for them, and re-layouts: 0.03 us -> 4.68 us
  transfers between devices with their start and end apart: 8 -> 2, of which waited for: 8 -> 0; matrix products, arithmetic and copies ran while one was open for 10% -> 4% of each run, Pallas kernels for 0% -> 0%
where the time goes in v2:
time: 262 us; the launch traced here: 258 us
  Pallas kernels  196 us (75%)
  matrix products  28.2 us (11%)
  other arithmetic  15.6 us (6%)
  local copies, waits for them, and re-layouts  11.5 us (4%)
  starting transfers between devices  6.24 us (2%)
    pallas_call x1, Pallas kernels, gather_inputs(): pl.pallas_call(gather_kernel, out_shape=(jax.ShapeDtypeStruct((4 * tokens...  110 us
    pallas_call x1, Pallas kernels, project_out(): pl.pallas_call(project_kernel, out_shape=jax.ShapeDtypeStruct((Z_SIZE * p...  86 us
    dot_general x2, matrix products, add_rows(): return jnp.dot(normalized_rows, weights, preferred_element_type=jnp.float32)  13.5 us
    sub x1, matrix products, attend(): weights = jnp.where(allowed[None, None], jnp.exp(scores - row_max), 0.0)  10.9 us
    ppermute x2, starting transfers between devices, shifted(): lax.ppermute(value, axis, [(source, source + steps) for source in range(l...  6.24 us
  transfers between devices with their start and end apart: 2, of which 0 were waited for; matrix products, arithmetic and copies ran while one was open for 4% of the time, Pallas kernels for 0%

profile of v2, /device:TPU:0, one launch (start us, length us, event | category | flops | bytes accessed | tf_op | source)
XLA Modules:
  0.0 258.2 jit_solution(8278401015054012206)
XLA Ops:
  0.0 1.8 copy.24
  1.8 0.7 fusion.13
  2.6 2.3 fusion.15
  4.9 1.5 copy.25.x_ref
  6.4 110.3 %gather_inputs.1 = (bf16[512,5376]{1,0:T(8,128)(2,1)}, bf16[5376,1024]{1,0:T(8,128)(2,1)}) custom-call(bf16[128,5376]{1,0:T(8,128)(2,1)} %copy.25.x_ref, bf16[672,512]{1,0:T(8,128)(2,1)} %q_ref.1, bf16[672,256]{1,0:T(8,128)(2,1)} %k_ref.1, bf16[672,256]{1,0:T(8,128)(2,1)} %v_ref.1), custom_call_target="tpu_custom_call" | custom-call | tf_op jit(solution)/shard_map/gather_inputs/pallas_call | solution.py:269
  116.7 6.7 %fusion.9 = f32[512,512]{0,1:T(8,128)S(1)} fusion(bf16[512,5376]{1,0:T(8,128)(2,1)} %get-tuple-element.7, bf16[5376,1024]{1,0:T(8,128)(2,1)} %get-tuple-element.8), kind=kOutput, calls=%fused_computation.11 | convolution fusion | flops 2818572288 | bytes 12058624 | tf_op jit(solution)/shard_map/dot_general | solution.py:459
  124.1 0.6 broadcast_subtract_fusion
  124.9 0.5 multiply_cosine_fusion
  126.5 1.0 pad_maximum_fusion
  127.5 3.9 %collective-permute-start.1 = (bf16[2,512,2,128]{3,1,2,0:T(8,128)(2,1)}, bf16[2,512,2,128]{3,1,2,0:T(8,128)(2,1)}, u32[]{:S(2)}, u32[]{:S(2)}) collective-permute-start(bf16[2,512,2,128]{3,1,2,0:T(8,128)(2,1)} %pad_maximum_fusion), channel_id=1, source_target_pairs={{0,4},{4,8},{8,12},{12,16},{16,20},{20,24},{24,28},{1,5},{5,9},{9,... | collective-permute-start | bytes 1572872 | tf_op jit(solution)/shard_map/ppermute | solution.py:20
  131.3 2.4 collective-permute-start
  133.7 6.7 %multiply_reduce_fusion.1 = (f32[512,4]{0,1:T(4,128)S(1)}, f32[512,512]{0,1:T(8,128)S(1)}) fusion(bf16[512,5376]{1,0:T(8,128)(2,1)} %get-tuple-element.7, bf16[5376,1024]{1,0:T(8,128)(2,1)} %get-tuple-element.8), kind=kOutput, calls=%fused_computation.31 | convolution fusion | flops 2819094528 | bytes 12066816 | tf_op jit(solution)/shard_map/dot_general | solution.py:459
  141.3 1.0 copy.31
  142.3 2.0 fusion.12
  144.3 2.5 maximum_maximum_fusion
  146.8 10.9 %fusion.38 = (f32[2,2,512]{2,1,0:T(2,128)S(1)}, bf16[2,2,512,1536]{2,3,1,0:T(8,128)(2,1)}) fusion(pred[512,1536]{0,1:T(8,128)(4,1)} %fusion.12, bf16[2,1536,2,128]{3,1,2,0:T(8,128)(2,1)} %maximum_maximum_fusion, bf16[512,2,2,64]{3,0,2,1:T(8,128)(2,1)} %bitcast.75, bf16[512,2,2,64]{3,0,2,1:T(8,128)(2,1)S(1)} %bitcast.74), kind=kOutput, calls=%fused_computation.63 | convolution fusion | flops 825230848 | bytes 9183232 | tf_op jit(solution)/shard_map/sub | solution.py:421
  157.8 3.8 %fusion.25 = bf16[512,2,2,128]{0,3,2,1:T(8,128)(2,1)S(1)} fusion(bf16[2,2,512,1536]{2,3,1,0:T(8,128)(2,1)} %get-tuple-element.22, bf16[2,1536,2,128]{3,1,2,0:T(8,128)(2,1)S(1)} %copy-done.1, f32[512,2,2]{0,2,1:T(2,128)S(1)} %bitcast.76), kind=kOutput, calls=%fused_computation.29 | convolution fusion | flops 805830656 | bytes 7610368 | tf_op jit(solution)/shard_map/kgqs,skd->qkgd/dot_general | solution.py:424
  161.7 1.1 constant_dynamic-slice_fusion
  162.8 1.5 copy.43
  164.4 1.3 copy.42
  165.7 86.0 %project_out.1 = f32[5376,128]{1,0:T(8,128)} custom-call(bf16[672,512]{1,0:T(8,128)(2,1)} %bitcast.73, bf16[256,512]{1,0:T(8,128)(2,1)} %bitcast.72, bf16[256,512]{1,0:T(8,128)(2,1)} %bitcast.71), custom_call_target="tpu_custom_call" | custom-call | tf_op jit(solution)/shard_map/project_out/pallas_call | solution.py:393
  251.7 2.7 %multiply_reduce_fusion = f32[128]{0:T(128)S(1)} fusion(f32[5376,128]{1,0:T(8,128)} %project_out.1), kind=kLoop, calls=%fused_computation.24 | loop fusion | flops 1376128 | bytes 2753024 | tf_op jit(solution)/shard_map/reduce_sum | solution.py:24
  254.3 2.3 fusion.16
  256.6 1.5 copy.36
  (38 shorter events, 2.7 us)
Async XLA Ops:
  0.0 2.6 copy-start.2
  116.7 6.9 %copy-start.4 = (s32[4096]{0:T(1024)S(1)}, s32[4096]{0:T(1024)}, u32[]{:S(2)}) copy-start(s32[4096]{0:T(1024)} %param.11) | copy-start | bytes 49156
  123.4 2.6 %copy-start.5 = (f32[128]{0:T(128)S(1)}, f32[128]{0:T(128)}, u32[]{:S(2)}) copy-start(f32[128]{0:T(128)} %param.18) | copy-start | bytes 1540
  127.5 13.1 %copy-start.6 = (f32[128]{0:T(128)S(1)}, f32[128]{0:T(128)}, u32[]{:S(2)}) copy-start(f32[128]{0:T(128)} %param.17) | copy-start | bytes 1540
  127.5 16.8 %collective-permute-start.1 = (bf16[2,512,2,128]{3,1,2,0:T(8,128)(2,1)}, bf16[2,512,2,128]{3,1,2,0:T(8,128)(2,1)}, u32[]{:S(2)}, u32[]{:S(2)}) collective-permute-start(bf16[2,512,2,128]{3,1,2,0:T(8,128)(2,1)} %pad_maximum_fusion), channel_id=1, source_target_pairs={{0,4},{4,8},{8,12},{12,16},{16,20},{20,24},{24,28},{1,5},{5,9},{9,... | collective-permute-start | bytes 1572872 | tf_op jit(solution)/shard_map/ppermute | solution.py:20
  131.3 12.9 %collective-permute-start = (bf16[2,512,2,128]{3,1,2,0:T(8,128)(2,1)}, bf16[2,512,2,128]{3,1,2,0:T(8,128)(2,1)}, u32[]{:S(2)}, u32[]{:S(2)}) collective-permute-start(bf16[2,512,2,128]{3,1,2,0:T(8,128)(2,1)} %pad_maximum_fusion), channel_id=1, source_target_pairs={{0,8},{4,12},{8,16},{12,20},{16,24},{20,28},{1,9},{5,13},{9,17},{1... | collective-permute-start | bytes 1572872 | tf_op jit(solution)/shard_map/ppermute | solution.py:20
  146.8 10.9 %copy-start.1 = (bf16[2,1536,2,128]{3,1,2,0:T(8,128)(2,1)S(1)}, bf16[2,1536,2,128]{3,1,2,0:T(8,128)(2,1)}, u32[]{:S(2)}) copy-start(bf16[2,1536,2,128]{3,1,2,0:T(8,128)(2,1)} %maximum_maximum_fusion) | copy-start | bytes 4718596
  165.7 88.6 %copy-start.3 = (f32[5376]{0:T(1024)S(1)}, f32[5376]{0:T(1024)}, u32[]{:S(2)}) copy-start(f32[5376]{0:T(1024)} %param.19) | copy-start | bytes 64516
  251.7 2.7 %copy-start = (f32[5376,128]{1,0:T(8,128)S(1)}, f32[5376,128]{1,0:T(8,128)}, u32[]{:S(2)}) copy-start(f32[5376,128]{1,0:T(8,128)} %project_out.1) | copy-start | bytes 8257540
